TPU v7x, 256 devices: a whole 4x4x8 slice. The times are simulated.
256 devices in a mesh: heads: 8 (over y_lo, x), ctx: 32 (over z, y_hi, core).
Axes of the slice: x: 4, y: 4 (y_hi: 2, y_lo: 2; y = y_hi * 2 + y_lo), z: 8, core: 2. Of those that a mesh axis runs over, the one named last changes fastest.
Arguments:
- queries: bfloat16 [12288, 8192], P('ctx', 'heads'), may hold values from -20 to 20
- keys: bfloat16 [12288, 1024], P('ctx', 'heads'), may hold values from -20 to 20
- values: bfloat16 [12288, 1024], P('ctx', 'heads'), may hold values from -6 to 6
- positions: int32 [12288], P('ctx'), may hold values from 0 to 18431, as said below
Outputs:
- attended: bfloat16 [12288, 8192], P(('ctx', 'heads'))
Inputs may be any that keep to these rules, and one draw needn't show every extreme that they name: `positions`: positions start at 0 at the first token and rise by 1 or 2 from each token to the next; exactly 6144 of these steps rise by 2.
All inputs are finite; a program needn't handle non-finite values.
Results may differ from a plain program's by a relative error of at most 0.0092.
Values may be sent and summed in bfloat16 or wider, within the bound.
A program may use at most 64 MiB of HBM per device.

v0:
```python
import math

import jax
import jax.numpy as jnp
from jax import lax
from jax.sharding import PartitionSpec as P

HD = 128


NEG_FILL = -1e30


def in_one_piece(arrays, axis, dim, along):
    ends, at = ([], 0)
    for a in arrays[:-1]:
        at += a.shape[along]
        ends.append(at)
    both = jnp.concatenate(arrays, axis=along)
    return tuple(jnp.split(lax.all_gather(both, axis, axis=dim, tiled=True), ends, axis=along))


def rotary_tables(positions, head_dim):
    step_index = jnp.arange(head_dim // 2, dtype=jnp.float32)
    base_freq = jnp.power(jnp.float32(500000.0), -(2.0 * step_index / head_dim))
    wavelen = 2.0 * math.pi / base_freq
    blend_factor = (8192.0 / wavelen - 1.0) / 3.0
    middle = (1.0 - blend_factor) * base_freq / 8.0 + blend_factor * base_freq
    inv_freq = jnp.where(
        wavelen < 2048.0, base_freq, jnp.where(wavelen > 8192.0, base_freq / 8.0, middle)
    )
    angles = positions.astype(jnp.float32)[:, None] * inv_freq[None, :]
    return (jnp.cos(angles), jnp.sin(angles))


def rotate(head_data, cosine, sine_table):
    halfway = head_data.shape[-1] // 2
    first_part = head_data[..., :halfway]
    second = head_data[..., halfway:]
    cos_rows = cosine[:, None, :]
    sin_rows = sine_table[:, None, :]
    return jnp.concatenate(
        [first_part * cos_rows - second * sin_rows, second * cos_rows + first_part * sin_rows],
        axis=-1,
    )


def attend_piece(
    carry_now, queries_part, query_rows, keys_part, values_part, key_start, scale_value
):
    rows_count = queries_part.shape[0]
    keys_count = keys_part.shape[0]

    def update(state_now):
        prev_max, prev_sum, prev_acc = state_now
        scores = (
            jnp.einsum(
                "qhgd,khd->hgqk", queries_part, keys_part, preferred_element_type=jnp.float32
            )
            * scale_value
        )
        query_index = jnp.broadcast_to(query_rows[:, None], (rows_count, keys_count))
        key_index = key_start + lax.broadcasted_iota(jnp.int32, (rows_count, keys_count), 1)
        allowed = key_index <= query_index
        scores = jnp.where(allowed, scores, NEG_FILL)
        new_max = jnp.maximum(prev_max, jnp.max(scores, axis=-1))
        weights = jnp.where(allowed, jnp.exp(scores - new_max[..., None]), 0.0)
        factor = jnp.exp(prev_max - new_max)
        new_sum = prev_sum * factor + jnp.sum(weights, axis=-1)
        mixed_values = jnp.einsum(
            "hgqk,khd->hgqd",
            weights.astype(jnp.bfloat16),
            values_part,
            preferred_element_type=jnp.float32,
        )
        return (new_max, new_sum, prev_acc * factor[..., None] + mixed_values)

    return lax.cond(
        key_start <= jnp.max(query_rows), update, lambda state_now: state_now, carry_now
    )


def local(queries, keys, values, positions):
    tok_rows = queries.shape[0]
    kv_local = keys.shape[1] // HD
    group_size = queries.shape[1] // (kv_local * HD)
    halfway = tok_rows // 2
    ctx_rank = lax.axis_index("ctx")
    scale_value = 1.0 / math.sqrt(HD)
    cosine, sine_table = rotary_tables(positions, HD)
    rot_queries = rotate(
        queries.astype(jnp.float32).reshape(tok_rows, kv_local * group_size, HD), cosine, sine_table
    )
    rot_queries = rot_queries.astype(jnp.bfloat16).reshape(tok_rows, kv_local, group_size, HD)
    rot_keys = rotate(
        keys.astype(jnp.float32).reshape(tok_rows, kv_local, HD), cosine, sine_table
    ).astype(jnp.bfloat16)
    flat_keys = rot_keys.reshape(tok_rows, kv_local * HD)
    half_iota = jnp.arange(halfway, dtype=jnp.int32)
    first_queries = rot_queries[:halfway]
    second_queries = rot_queries[halfway:]
    first_rows = ctx_rank * tok_rows + half_iota
    second_rows = ctx_rank * tok_rows + halfway + half_iota

    def fresh_state():
        return (
            jnp.full((kv_local, group_size, halfway), NEG_FILL, jnp.float32),
            jnp.zeros((kv_local, group_size, halfway), jnp.float32),
            jnp.zeros((kv_local, group_size, halfway, HD), jnp.float32),
        )

    pieces = in_one_piece((flat_keys, values), "ctx", 0, 1)
    piece_rows = pieces[0].shape[0]
    block_rows = math.gcd(piece_rows, 512)

    def one_block(block_index, inner_carry):
        offset = block_index * block_rows
        key_block = lax.dynamic_slice_in_dim(pieces[0], offset, block_rows, 0).reshape(
            block_rows, kv_local, HD
        )
        value_block = lax.dynamic_slice_in_dim(pieces[1], offset, block_rows, 0).reshape(
            block_rows, kv_local, HD
        )
        first_state = attend_piece(
            inner_carry[0], first_queries, first_rows, key_block, value_block, offset, scale_value
        )
        second_state = attend_piece(
            inner_carry[1], second_queries, second_rows, key_block, value_block, offset, scale_value
        )
        return (first_state, second_state)

    states = lax.fori_loop(0, piece_rows // block_rows, one_block, (fresh_state(), fresh_state()))

    def finish(state_now):
        run_acc = state_now[2] / state_now[1][..., None]
        return (
            jnp.transpose(run_acc, (2, 0, 1, 3))
            .reshape(halfway, kv_local * group_size * HD)
            .astype(jnp.bfloat16)
        )

    first_out = finish(states[0])
    second_out = finish(states[1])
    combined = jnp.concatenate([first_out, second_out], axis=0)
    return lax.all_to_all(combined, "heads", split_axis=0, concat_axis=1, tiled=True)


def solution(mesh):
    return jax.shard_map(
        local,
        mesh=mesh,
        in_specs=(P("ctx", "heads"), P("ctx", "heads"), P("ctx", "heads"), P("ctx")),
        out_specs=P(("ctx", "heads"), None),
        check_vma=False,
    )
```

profile of v0, /device:TPU:241, one launch (start us, length us, event | category | flops | bytes accessed | tf_op | source)
XLA Modules:
  0.0 353.6 jit_solution(1305402511884951156)
XLA Ops:
  9.0 1.7 pad_maximum_fusion.2
  10.7 1.5 copy.10
  14.5 86.7 %all-gather.2.cloned.1.call-done = bf16[12288,256]{1,0:T(8,128)(2,1)} async-done(((bf16[384,256]{1,0:T(8,128)(2,1)}), bf16[12288,256]{1,0:T(8,128)(2,1)}) %all-gather.2.cloned.1.call-update) | async-done | bytes 6291472 | tf_op jit(solution)/shard_map/all_gather | solution.py:20
  101.2 4.7 %fusion.61 = (bf16[12288,128]{1,0:T(8,128)(2,1)}, bf16[12288,128]{1,0:T(8,128)(2,1)}) fusion(bf16[12288,256]{1,0:T(8,128)(2,1)} %all-gather.2.cloned.1.call-done), kind=kLoop, calls=%fused_computation.87 | loop fusion | bytes 12582912 | tf_op jit(solution)/shard_map/split | solution.py:20
  106.0 222.5 %while.25 = (s32[]{:T(128)}, f32[1,8,192]{2,1,0:T(8,128)S(1)}, f32[1,8,192]{2,1,0:T(8,128)S(1)}, f32[1,8,192,128]{3,2,1,0:T(8,128)S(1)}, f32[1,8,192]{2,1,0:T(8,...) while((s32[]{:T(128)}, f32[1,8,192]{2,1,0:T(8,128)S(1)}, ...), condition=%wide.region_11.12_spmd.clone, body=%wide.region_2.11_spmd.clone.sunk | while | flops 826747264 | bytes 24853004 | solution.py:132
  108.3 3.5 conditional.6
  111.8 3.5 conditional.7
  117.6 3.5 conditional.6
  119.6 1.4 fusion.14
  121.1 3.5 conditional.7
  126.8 3.5 conditional.6
  128.9 1.4 fusion.14
  130.4 3.5 conditional.7
  136.1 3.5 conditional.6
  138.1 1.4 fusion.14
  139.6 3.5 conditional.7
  145.4 3.5 conditional.6
  148.9 3.5 conditional.7
  154.7 3.5 conditional.6
  158.2 3.5 conditional.7
  163.9 3.5 conditional.6
  167.4 3.5 conditional.7
  173.2 3.5 conditional.6
  175.2 1.4 fusion.14
  176.7 3.5 conditional.7
  182.5 3.5 conditional.6
  184.5 1.4 fusion.14
  186.0 3.5 conditional.7
  191.7 3.5 conditional.6
  193.8 1.4 fusion.14
  195.3 3.5 conditional.7
  201.0 3.5 conditional.6
  203.0 1.4 fusion.14
  204.5 3.5 conditional.7
  210.3 3.5 conditional.6
  212.3 1.4 fusion.14
  213.8 3.5 conditional.7
  219.6 3.5 conditional.6
  221.6 1.4 fusion.14
  223.1 3.5 conditional.7
  228.8 3.5 conditional.6
  230.9 1.4 fusion.14
  232.3 3.5 conditional.7
  238.1 3.5 conditional.6
  241.6 3.5 conditional.7
  247.4 3.5 conditional.6
  250.9 3.5 conditional.7
  256.7 3.5 conditional.6
  260.2 3.5 conditional.7
  265.9 3.5 conditional.6
  269.4 3.5 conditional.7
  275.2 3.5 conditional.6
  278.7 3.5 conditional.7
  284.5 3.5 conditional.6
  288.0 3.5 conditional.7
  293.7 3.5 conditional.6
  297.2 3.5 conditional.7
  303.0 3.5 conditional.6
  306.5 3.5 conditional.7
  312.3 3.5 conditional.6
  315.8 3.5 conditional.7
  321.6 3.5 conditional.6
  325.1 3.5 conditional.7
  329.9 16.0 %all_to_all.19 = bf16[8,48,1024]{2,1,0:T(8,128)(2,1)S(1)} all-to-all(bf16[8,48,1024]{2,1,0:T(8,128)(2,1)S(1)} %bitcast.151), channel_id=1, replica_groups=mesh['heads'=8,'ctx'=32] {'heads'}, dimensions={0} | all-to-all | bytes 1572864 | tf_op jit(solution)/shard_map/all_to_all | solution.py:145
  (521 shorter events, 181.1 us)
Async XLA Ops:
  6.5 94.6 %all-gather.2.cloned.1.call-start = ((), (), s32[]{:S(2)}) async-start(), calls=%async_computation.1 | async-start | bytes 6488064 | tf_op jit(solution)/shard_map/all_gather | solution.py:20
Sparse Core Ops, SparseCore 0:
  10.8 90.2 all-gather.1
where the time goes:
time: 355 us; the launch traced here: 354 us
  matrix products  104 us (29%)
  waiting for transfers between devices  86.7 us (24%)
  other arithmetic  66.4 us (19%)
  loops' own time  34 us (10%)
  local copies, waits for them, and re-layouts  32.6 us (9%)
  blocking collectives  16 us (5%)
  between operations  13.5 us (4%)
    all_gather x1, waiting for transfers between devices, in_one_piece(): lax.all_gather(both, axis, axis=dim, tiled=True)  86.7 us
    dot_general x48, matrix products, update(): jnp.einsum('hgqk,khd->hgqd', weights.astype(jnp.bfloat16), values_part, p...  69 us
    reduce_sum x48, other arithmetic, update(): new_sum = prev_sum * factor + jnp.sum(weights, axis=-1)  52.6 us
    dot_general x48, matrix products, update(): jnp.einsum('qhgd,khd->hgqk', queries_part, keys_part, preferred_element_t...  35.5 us
    another operation x1, loops' own time, local(): lax.fori_loop(0, piece_rows // block_rows, one_block, (fresh_state(), fre...  30.9 us
    reshape x24, local copies, waits for them, and re-layouts, one_block(): lax.dynamic_slice_in_dim(pieces[1], offset, block_rows, 0)  23.8 us
    all_to_all x1, blocking collectives, local(): lax.all_to_all(combined, 'heads', split_axis=0, concat_axis=1, tiled=True)  16 us
  transfers between devices with their start and end apart: 1, of which 1 were waited for; matrix products, arithmetic and copies ran while one was open for 1% of the time, Pallas kernels for 0%

commit v1 on v0

v1 whole, which is shorter than its diff:
```python
import functools
import math

import jax
import jax.numpy as jnp
from jax import lax
from jax.experimental import pallas as pl
from jax.experimental.pallas import tpu as pltpu
from jax.sharding import PartitionSpec as P

HD = 128
NEG_FILL = -1e30
MESH = pl.DeviceIdType.MESH
SLABS = 8
WIDE = 4
SEQ = 7


def rotary_tables(positions, head_dim):
    step_index = jnp.arange(head_dim // 2, dtype=jnp.float32)
    base_freq = jnp.power(jnp.float32(500000.0), -(2.0 * step_index / head_dim))
    wavelen = 2.0 * math.pi / base_freq
    blend_factor = (8192.0 / wavelen - 1.0) / 3.0
    middle = (1.0 - blend_factor) * base_freq / 8.0 + blend_factor * base_freq
    inv_freq = jnp.where(
        wavelen < 2048.0, base_freq, jnp.where(wavelen > 8192.0, base_freq / 8.0, middle)
    )
    angles = positions.astype(jnp.float32)[:, None] * inv_freq[None, :]
    return (jnp.cos(angles), jnp.sin(angles))


def rotate(head_data, cosine, sine_table):
    halfway = head_data.shape[-1] // 2
    first_part = head_data[..., :halfway]
    second = head_data[..., halfway:]
    cos_rows = cosine[:, None, :]
    sin_rows = sine_table[:, None, :]
    return jnp.concatenate(
        [first_part * cos_rows - second * sin_rows, second * cos_rows + first_part * sin_rows],
        axis=-1,
    )


def attend_kernel(
    heads_n,
    q_ref,
    kv_ref,
    out_ref,
    kv_all,
    q_far,
    q_two,
    acc,
    total,
    top,
    stage,
    own_sem,
    side_sem,
    recv_sem,
    up_sem,
    down_sem,
    core_sem,
    q_sem,
    out_send,
    out_recv,
):
    rows = q_ref.shape[0]
    half = q_ref.shape[1] // 2
    tiles = half // HD
    share = rows // heads_n
    scale = math.log2(math.e) / math.sqrt(HD)
    head = lax.axis_index("heads")
    rank = lax.axis_index("ctx")
    ranks = SLABS * WIDE
    z = rank // WIDE
    place = rank % WIDE
    across = (place + 2) % WIDE
    far = ranks - 1 - rank
    mate = rank + 1 - 2 * (rank % 2)
    other = z * WIDE + across
    up = (rank + WIDE) % ranks
    down = (rank + ranks - WIDE) % ranks

    barrier = pltpu.get_barrier_semaphore()
    for peer in (mate, other, up, down):
        pl.semaphore_signal(barrier, inc=1, device_id={"ctx": peer}, device_id_type=MESH)
    for hop in range(heads_n):
        peer = (head + hop) % heads_n
        pl.semaphore_signal(
            barrier, inc=1, device_id={"heads": peer, "ctx": far}, device_id_type=MESH
        )
        if hop:
            pl.semaphore_signal(
                barrier, inc=1, device_id={"heads": peer, "ctx": rank}, device_id_type=MESH
            )
    pl.semaphore_wait(barrier, 3 + 2 * heads_n)

    def send(source, slot, peer, sem):
        return pltpu.make_async_remote_copy(
            src_ref=source,
            dst_ref=kv_all.at[slot],
            send_sem=sem,
            recv_sem=recv_sem.at[slot],
            device_id={"ctx": peer},
            device_id_type=MESH,
        )

    def arrived(slot):
        send(kv_all.at[slot], slot, mate, core_sem.at[0]).wait_recv()

    def incoming(k, upward):
        odd = k % 2
        if upward:
            mine = jnp.logical_or(odd == 1, k == 0)
            dist = jnp.where(mine, jnp.where(k == 0, 1, (k + 3) // 2), k // 2)
            slab = (z + SLABS - dist) % SLABS
            onward = jnp.where(mine, dist < 4, dist < 3)
        else:
            mine = jnp.logical_and(jnp.logical_or(odd == 1, k == 0), k < 5)
            dist = jnp.where(
                k >= 5, k - 2, jnp.where(mine, jnp.where(k == 0, 1, (k + 3) // 2), k // 2)
            )
            slab = (z + dist) % SLABS
            onward = jnp.where(mine, dist < 3, dist < 4)
        return slab * WIDE + jnp.where(mine, place, across), onward

    def relay(k):
        for upward in (True, False):
            slot, onward = incoming(k, upward)
            arrived(slot)

            @pl.when(onward)
            def _():
                if upward:
                    send(kv_all.at[slot], slot, up, up_sem.at[k + 2]).start()
                else:
                    send(kv_all.at[slot], slot, down, down_sem.at[k + 2]).start()

            send(kv_all.at[slot], slot, mate, core_sem.at[2 + 2 * k + int(upward)]).start()

    send(kv_ref, rank, up, up_sem.at[0]).start()
    send(kv_ref, rank, down, down_sem.at[0]).start()
    send(kv_ref, rank, other, side_sem.at[0]).start()
    send(kv_ref, rank, mate, core_sem.at[0]).start()
    own = pltpu.make_async_copy(kv_ref, kv_all.at[rank], own_sem.at[0])
    own.start()
    far_copy = pltpu.make_async_remote_copy(
        src_ref=q_ref.at[:, pl.ds(half, half)],
        dst_ref=q_far,
        send_sem=q_sem.at[0],
        recv_sem=q_sem.at[1],
        device_id={"ctx": far},
        device_id_type=MESH,
    )
    far_copy.start()

    def split_queries(source, g):
        for t in range(tiles):
            wide = source[:, t * HD : (t + 1) * HD].astype(jnp.float32) * scale
            high = wide.astype(jnp.bfloat16)
            q_two[g, t, :, :HD] = high
            q_two[g, t, :, HD:] = (wide - high.astype(jnp.float32)).astype(jnp.bfloat16)

    acc[...] = jnp.zeros_like(acc)
    total[...] = jnp.zeros_like(total)
    top[...] = jnp.full_like(top, NEG_FILL)
    split_queries(q_ref, 0)

    relay(0)
    arrived(other)
    send(kv_all.at[other], other, up, up_sem.at[1]).start()
    send(kv_all.at[other], other, down, down_sem.at[1]).start()
    send(kv_all.at[other], other, mate, core_sem.at[1]).start()
    own.wait()

    def slab_of(s):
        dist = (s + 1) // 2
        return jnp.where(s % 2 == 1, z + SLABS - dist, jnp.where(s == 7, z + 4, z + dist)) % SLABS

    def last_step(limit):
        last = 0
        for s in range(SLABS):
            last = jnp.where(slab_of(s) <= limit, s, last)
        return last

    last_own = last_step(z)
    last_far = last_step(SLABS - 1 - z)

    def body(slab, g, offset):
        keys = kv_all[pl.ds(slab * WIDE, WIDE), 0].reshape(WIDE * rows, HD)
        vals = kv_all[pl.ds(slab * WIDE, WIDE), 1].reshape(WIDE * rows, HD)
        keys = jnp.concatenate([keys, keys], axis=1)
        vals = jnp.concatenate([vals, jnp.ones_like(vals)], axis=1)
        scores = [
            lax.dot_general(
                q_two[g, t],
                keys,
                (((1,), (1,)), ((), ())),
                preferred_element_type=jnp.float32,
            )
            for t in range(tiles)
        ]
        if offset is not None:
            shape = (rows, WIDE * rows)
            ahead = lax.broadcasted_iota(jnp.int32, shape, 1) - lax.broadcasted_iota(
                jnp.int32, shape, 0
            )
            allowed = ahead <= offset
            scores = [jnp.where(allowed, s, NEG_FILL) for s in scores]
        for t in range(tiles):
            before = top[g, t]
            now = jnp.maximum(before, jnp.max(scores[t], axis=1, keepdims=True))
            weights = jnp.exp2(scores[t] - now[:, :1]).astype(jnp.bfloat16)
            fade = jnp.exp2(before - now)
            top[g, t] = now
            mixed = lax.dot_general(
                weights, vals, (((1,), (0,)), ((), ())), preferred_element_type=jnp.float32
            )
            acc[g, t] = acc[g, t] * fade + mixed[:, :HD]
            total[g, t] = total[g, t] * fade + mixed[:, HD:]

    def piece(g, hop, owner):
        peer = (head + hop) % heads_n
        column = pl.multiple_of(head * (2 * half) + g * half, half)
        return pltpu.make_async_remote_copy(
            src_ref=stage.at[g, pl.ds(peer * share, share)],
            dst_ref=out_ref.at[:, pl.ds(column, half)],
            send_sem=out_send.at[g, hop],
            recv_sem=out_recv.at[g, hop],
            device_id={"heads": peer, "ctx": owner},
            device_id_type=MESH,
        )

    def own_piece():
        column = pl.multiple_of(head * (2 * half), half)
        return pltpu.make_async_copy(
            stage.at[0, pl.ds(head * share, share)],
            out_ref.at[:, pl.ds(column, half)],
            own_sem.at[1],
        )

    def finish(g):
        for t in range(tiles):
            stage[g, :, t * HD : (t + 1) * HD] = (acc[g, t] / total[g, t]).astype(stage.dtype)

    def step(i, carry):
        s, g = i // 2, i % 2
        slab = slab_of(s)
        k = jnp.where(i == 1, 1, s + 1)

        @pl.when(jnp.logical_or(i == 1, jnp.logical_and(g == 0, jnp.logical_and(s >= 1, k < SEQ))))
        def _():
            relay(k)

        @pl.when(i == 1)
        def _():
            far_copy.wait_recv()
            split_queries(q_far, 1)

        @pl.when(g == 0)
        def _():
            for y in range(2):
                arrived(slab * WIDE + 2 * y + (1 - rank % 2))

        limit = jnp.where(g == 0, z, SLABS - 1 - z)
        owner = jnp.where(g == 0, rank, far)

        @pl.when(slab < limit)
        def _():
            body(slab, g, None)

        @pl.when(slab == limit)
        def _():
            body(slab, g, (owner % WIDE) * rows)

        @pl.when(jnp.logical_and(g == 0, s == last_own))
        def _():
            finish(0)
            for hop in range(1, heads_n):
                piece(0, hop, rank).start()
            own_piece().start()

        @pl.when(jnp.logical_and(g == 1, s == last_far))
        def _():
            finish(1)
            for hop in range(heads_n):
                piece(1, hop, far).start()

        return carry

    lax.fori_loop(0, 2 * SLABS, step, 0)

    own_piece().wait()
    for hop in range(heads_n):
        if hop:
            piece(0, hop, rank).wait_send()
            piece(0, hop, rank).wait_recv()
        piece(1, hop, far).wait_send()
        piece(1, hop, far).wait_recv()
    far_copy.wait_send()
    send(kv_ref, rank, other, side_sem.at[0]).wait_send()
    for n in range(2 + 2 * SEQ):
        send(kv_ref, rank, mate, core_sem.at[n]).wait_send()
    for n in (0, 1, 2, 3, 4, 5, 6):
        send(kv_ref, rank, up, up_sem.at[n]).wait_send()
    for n in (0, 1, 2, 3, 4, 6, 7):
        send(kv_ref, rank, down, down_sem.at[n]).wait_send()


def local(heads_n, queries, keys, values, positions):
    rows = queries.shape[0]
    group = queries.shape[1] // HD
    cosine, sine_table = rotary_tables(positions, HD)
    rot_q = rotate(queries.astype(jnp.float32).reshape(rows, group, HD), cosine, sine_table)
    rot_q = rot_q.astype(jnp.bfloat16).reshape(rows, group * HD)
    rot_k = rotate(keys.astype(jnp.float32).reshape(rows, 1, HD), cosine, sine_table)
    rot_k = rot_k.astype(jnp.bfloat16).reshape(rows, HD)
    both = jnp.stack([rot_k, values])
    tiles = group // 2
    ranks = SLABS * WIDE
    vmem = pl.BlockSpec(memory_space=pltpu.VMEM)
    dma = pltpu.SemaphoreType.DMA
    return pl.pallas_call(
        functools.partial(attend_kernel, heads_n),
        out_shape=jax.ShapeDtypeStruct((rows // heads_n, heads_n * group * HD), jnp.bfloat16),
        in_specs=[vmem, vmem],
        out_specs=vmem,
        scratch_shapes=[
            pltpu.VMEM((ranks, 2, rows, HD), jnp.bfloat16),
            pltpu.VMEM((rows, tiles * HD), jnp.bfloat16),
            pltpu.VMEM((2, tiles, rows, 2 * HD), jnp.bfloat16),
            pltpu.VMEM((2, tiles, rows, HD), jnp.float32),
            pltpu.VMEM((2, tiles, rows, HD), jnp.float32),
            pltpu.VMEM((2, tiles, rows, HD), jnp.float32),
            pltpu.VMEM((2, rows, tiles * HD), jnp.bfloat16),
            dma((2,)),
            dma((1,)),
            dma((ranks,)),
            dma((SEQ + 2,)),
            dma((SEQ + 2,)),
            dma((2 + 2 * SEQ,)),
            dma((2,)),
            dma((2, heads_n)),
            dma((2, heads_n)),
        ],
        compiler_params=pltpu.CompilerParams(
            collective_id=0, has_side_effects=True, vmem_limit_bytes=60000 * 1024
        ),
    )(rot_q, both)


def solution(mesh):
    return jax.shard_map(
        functools.partial(local, mesh.shape["heads"]),
        mesh=mesh,
        in_specs=(P("ctx", "heads"), P("ctx", "heads"), P("ctx", "heads"), P("ctx")),
        out_specs=P(("ctx", "heads"), None),
        check_vma=False,
    )
```

time: 355 us -> 107 us (0.30)
  the two profiles are of different devices: /device:TPU:241 before, /device:TPU:65 now
where the time goes in v1:
time: 107 us
  Pallas kernels  97.5 us (91%)
  other arithmetic  5.48 us (5%)
  local copies, waits for them, and re-layouts  3.48 us (3%)
    pallas_call x1, Pallas kernels, local(): pl.pallas_call(functools.partial(attend_kernel, heads_n), out_shape=jax.S...  97.5 us
    unnamed x7, local copies, waits for them, and re-layouts  3.48 us

profile of v1, /device:TPU:65, one launch (start us, length us, event | category | flops | bytes accessed | tf_op | source)
XLA Modules:
  0.0 106.5 jit_solution(13250203671457317473)
XLA Ops:
  0.0 0.7 convert_element_type.20
  0.7 0.8 multiply_cosine_fusion.1
  1.5 1.3 %convert_bitcast_fusion = f32[48,8,8,128]{3,1,2,0:T(8,128)S(1)} fusion(bf16[384,1024]{1,0:T(8,128)(2,1)} %param.4), kind=kLoop, calls=%fused_computation | loop fusion | flops 393216 | bytes 2359296
  2.8 0.3 copy.5
  3.1 0.6 subtract_convert_fusion
  3.8 0.0 copy-start
  3.8 0.4 pad_maximum_fusion
  4.2 0.0 copy-start.1
  4.2 1.1 %copy.8 = bf16[48,8,8,128]{3,1,2,0:T(8,128)(2,1)} copy(bf16[48,8,8,128]{3,2,1,0:T(8,128)(2,1)S(1)} %bitcast.17) | data formatting | bytes 1572864
  5.3 0.0 copy-done
  5.3 0.8 fusion.9
  6.2 0.0 copy-done.1
  6.2 0.8 pad_maximum_fusion.1.kv_ref
  7.0 97.5 %shard_map.46 = bf16[48,8192]{1,0:T(8,128)(2,1)} custom-call(bf16[384,1024]{1,0:T(8,128)(2,1)} %bitcast.16, bf16[2,384,128]{2,1,0:T(8,128)(2,1)} %pad_maximum_fusion.1.kv_ref), custom_call_target="tpu_custom_call" | custom-call | tf_op jit(solution)/shard_map/pallas_call | solution.py:322
  104.4 2.1 %copy.10 = bf16[48,8192]{1,0:T(8,128)(2,1)} copy(bf16[48,8192]{1,0:T(8,128)(2,1)} %shard_map.46) | data formatting | bytes 1572864
  (2 shorter events, 0.0 us)
Async XLA Ops:
  3.8 1.5 %copy-start = (bf16[384,128]{1,0:T(8,128)(2,1)S(1)}, bf16[384,128]{1,0:T(8,128)(2,1)}, u32[]{:S(2)}) copy-start(bf16[384,128]{1,0:T(8,128)(2,1)} %param.5) | copy-start | bytes 294916
  4.2 1.9 %copy-start.1 = (bf16[384,128]{1,0:T(8,128)(2,1)S(1)}, bf16[384,128]{1,0:T(8,128)(2,1)}, u32[]{:S(2)}) copy-start(bf16[384,128]{1,0:T(8,128)(2,1)} %param.6) | copy-start | bytes 294916

commit v2 on v1

v2 whole, which is shorter than its diff:
```python
import functools
import math

import jax
import jax.numpy as jnp
from jax import lax
from jax.experimental import pallas as pl
from jax.experimental.pallas import tpu as pltpu
from jax.sharding import PartitionSpec as P

HD = 128
NEG_FILL = -1e30
MESH = pl.DeviceIdType.MESH
SLABS = 8
WIDE = 4
LINE = 5


def rotary_tables(positions, head_dim):
    step_index = jnp.arange(head_dim // 2, dtype=jnp.float32)
    base_freq = jnp.power(jnp.float32(500000.0), -(2.0 * step_index / head_dim))
    wavelen = 2.0 * math.pi / base_freq
    blend_factor = (8192.0 / wavelen - 1.0) / 3.0
    middle = (1.0 - blend_factor) * base_freq / 8.0 + blend_factor * base_freq
    inv_freq = jnp.where(
        wavelen < 2048.0, base_freq, jnp.where(wavelen > 8192.0, base_freq / 8.0, middle)
    )
    angles = positions.astype(jnp.float32)[:, None] * inv_freq[None, :]
    return (jnp.cos(angles), jnp.sin(angles))


def attend_kernel(
    heads_n,
    q_ref,
    k_ref,
    v_ref,
    cos_ref,
    sin_ref,
    out_ref,
    kv_all,
    q_move,
    q_far,
    q_two,
    acc,
    total,
    top,
    stage,
    own_sem,
    recv_sem,
    up_sem,
    down_sem,
    side_sem,
    core_sem,
    q_send,
    q_recv,
    out_send,
    out_recv,
):
    rows = q_ref.shape[0]
    pair = 2 * HD
    pairs = q_ref.shape[1] // pair
    share = rows // heads_n
    scale = math.log2(math.e) / math.sqrt(HD)
    head = lax.axis_index("heads")
    rank = lax.axis_index("ctx")
    ranks = SLABS * WIDE
    z = rank // WIDE
    place = rank % WIDE
    across = (place + 2) % WIDE
    mate = rank + 1 - 2 * (rank % 2)
    other = z * WIDE + across
    up = (rank + WIDE) % ranks
    down = (rank + ranks - WIDE) % ranks
    helper = z == 0
    giver = z >= SLABS - 2
    sources = tuple((SLABS - 1 - n) * WIDE + place for n in range(2))

    def turn(x):
        wide = x.astype(jnp.float32)
        turned = wide * cos_ref[...] + pltpu.roll(wide, HD // 2, axis=1) * sin_ref[...]
        return turned.astype(jnp.bfloat16)

    kv_all[rank, 0] = turn(k_ref[...])
    kv_all[rank, 1] = v_ref[...]
    for t in range(2):
        column = (2 * pairs - 2 + t) * HD
        q_move[:, t * HD : (t + 1) * HD] = turn(q_ref[:, column : column + HD])

    barrier = pltpu.get_barrier_semaphore()
    for peer in (mate, other, up, down):
        pl.semaphore_signal(barrier, inc=1, device_id={"ctx": peer}, device_id_type=MESH)
    for hop in range(1, heads_n):
        peer = (head + hop) % heads_n
        pl.semaphore_signal(
            barrier, inc=1, device_id={"heads": peer, "ctx": rank}, device_id_type=MESH
        )

    def greet(ctx):
        for hop in range(heads_n):
            peer = (head + hop) % heads_n
            pl.semaphore_signal(
                barrier, inc=1, device_id={"heads": peer, "ctx": ctx}, device_id_type=MESH
            )

    @pl.when(helper)
    def _():
        for source in sources:
            greet(source)

    @pl.when(giver)
    def _():
        greet(place)

    more = jnp.where(helper, 2 * heads_n, jnp.where(giver, heads_n, 0))
    pl.semaphore_wait(barrier, 3 + heads_n + more)

    def send(source, slot, peer, sem):
        return pltpu.make_async_remote_copy(
            src_ref=source,
            dst_ref=kv_all.at[slot],
            send_sem=sem,
            recv_sem=recv_sem.at[slot],
            device_id={"ctx": peer},
            device_id_type=MESH,
        )

    def arrived(slot):
        send(kv_all.at[slot], slot, mate, core_sem.at[0]).wait_recv()

    def slot_at(shift, mine):
        return ((z + shift + SLABS) % SLABS) * WIDE + (place if mine else across)

    peers = {"up": (up, up_sem), "down": (down, down_sem), "side": (other, side_sem)}

    def relay(shift, mine, core_at, *onward):
        slot = slot_at(shift, mine)
        arrived(slot)
        for way, at in onward:
            peer, sem = peers[way]
            send(kv_all.at[slot], slot, peer, sem.at[at]).start()
        send(kv_all.at[slot], slot, mate, core_sem.at[core_at]).start()

    def event(n):
        if n == 0:
            relay(-1, True, 1, ("up", 1), ("side", 1))
            relay(1, True, 2, ("down", 1), ("side", 2))
            relay(0, False, 3)
        elif n == 1:
            relay(-2, True, 4, ("up", 2))
            relay(2, True, 5, ("down", 2))
            relay(-1, False, 6, ("up", 3))
        elif n == 2:
            relay(-3, True, 7, ("up", 4), ("side", 3))
            relay(3, True, 8)
            relay(1, False, 9, ("down", 3))
        elif n == 3:
            relay(2, False, 10, ("down", 4))
            relay(-2, False, 11)
        elif n == 4:
            relay(-4, True, 12, ("side", 4))
            relay(3, False, 13)
            relay(-3, False, 14)
        else:
            relay(-4, False, 15)

    mine = kv_all.at[rank]
    send(mine, rank, other, side_sem.at[0]).start()
    send(mine, rank, up, up_sem.at[0]).start()
    send(mine, rank, down, down_sem.at[0]).start()
    send(mine, rank, mate, core_sem.at[0]).start()

    def far_copy(n):
        return pltpu.make_async_remote_copy(
            src_ref=q_move,
            dst_ref=q_far.at[n],
            send_sem=q_send.at[n],
            recv_sem=q_recv.at[n],
            device_id={"ctx": place},
            device_id_type=MESH,
        )

    for n in range(2):

        @pl.when(z == SLABS - 1 - n)
        def _():
            far_copy(n).start()

    def split_queries(turned, at):
        wide = turned.astype(jnp.float32) * scale
        high = wide.astype(jnp.bfloat16)
        q_two[at, :, :HD] = high
        q_two[at, :, HD:] = (wide - high.astype(jnp.float32)).astype(jnp.bfloat16)

    acc[...] = jnp.zeros_like(acc)
    total[...] = jnp.zeros_like(total)
    top[...] = jnp.full_like(top, NEG_FILL)
    for t in range(2 * pairs):
        split_queries(turn(q_ref[:, t * HD : (t + 1) * HD]), t)

    def slab_of(s):
        n = jnp.maximum(s - 1, 0)
        dist = (n + 1) // 2
        return jnp.where(n % 2 == 1, z + SLABS - dist, jnp.where(n == 7, z + 4, z + dist)) % SLABS

    def last_step(limit):
        last = 1
        for s in range(2, SLABS + 1):
            last = jnp.where(slab_of(s) <= limit, s, last)
        return last

    lasts = (last_step(z), last_step(SLABS - 1), last_step(SLABS - 2))

    def body(first, width, base, tiles, offset):
        keys = kv_all[pl.ds(first, width), 0].reshape(width * rows, HD)
        vals = kv_all[pl.ds(first, width), 1].reshape(width * rows, HD)
        keys = jnp.concatenate([keys, keys], axis=1)
        vals = jnp.concatenate([vals, jnp.ones_like(vals)], axis=1)
        scores = [
            lax.dot_general(
                q_two[base + t],
                keys,
                (((1,), (1,)), ((), ())),
                preferred_element_type=jnp.float32,
            )
            for t in range(tiles)
        ]
        if offset is not None:
            shape = (rows, width * rows)
            ahead = lax.broadcasted_iota(jnp.int32, shape, 1) - lax.broadcasted_iota(
                jnp.int32, shape, 0
            )
            allowed = ahead <= offset
            scores = [jnp.where(allowed, s, NEG_FILL) for s in scores]
        for t in range(tiles):
            before = top[base + t]
            now = jnp.maximum(before, jnp.max(scores[t], axis=1, keepdims=True))
            weights = jnp.exp2(scores[t] - now[:, :1]).astype(jnp.bfloat16)
            fade = jnp.exp2(before - now)
            top[base + t] = now
            mixed = lax.dot_general(
                weights, vals, (((1,), (0,)), ((), ())), preferred_element_type=jnp.float32
            )
            acc[base + t] = acc[base + t] * fade + mixed[:, :HD]
            total[base + t] = total[base + t] * fade + mixed[:, HD:]

    def out_columns(p):
        return pl.ds(pl.multiple_of((head * pairs + p) * pair, pair), pair)

    def piece(at, p, hop, owner):
        peer = (head + hop) % heads_n
        return pltpu.make_async_remote_copy(
            src_ref=stage.at[at, pl.ds(peer * share, share)],
            dst_ref=out_ref.at[:, out_columns(p)],
            send_sem=out_send.at[at, hop],
            recv_sem=out_recv.at[p, hop],
            device_id={"heads": peer, "ctx": owner},
            device_id_type=MESH,
        )

    def own_piece(p):
        return pltpu.make_async_copy(
            stage.at[p, pl.ds(head * share, share)],
            out_ref.at[:, out_columns(p)],
            own_sem.at[p],
        )

    def finish(at):
        for t in range(2):
            tile = acc[2 * at + t] / total[2 * at + t]
            stage[at, :, t * HD : (t + 1) * HD] = tile.astype(stage.dtype)
        if at < pairs:
            for hop in range(1, heads_n):
                piece(at, at, hop, rank).start()
            own_piece(at).start()
        else:
            for hop in range(heads_n):
                piece(at, pairs - 1, hop, sources[at - pairs]).start()

    kept = jnp.where(giver, pairs - 1, pairs)

    def step(i, carry):
        s, item = i // 4, i % 4
        slab = slab_of(s)
        for n in range(6):

            @pl.when(i == (4, 5, 9, 13, 17, 21)[n])
            def _():
                event(n)

        @pl.when(jnp.logical_and(i == 6, helper))
        def _():
            for n in range(2):
                far_copy(n).wait_recv()
                for t in range(2):
                    split_queries(q_far[n, :, t * HD : (t + 1) * HD], 2 * (pairs + n) + t)

        @pl.when(i == 0)
        def _():
            arrived(mate)

        @pl.when(i == 4)
        def _():
            arrived(z * WIDE + 2 * (1 - place // 2) + 1 - place % 2)

        @pl.when(jnp.logical_and(s >= 2, item == 0))
        def _():
            for y in range(2):
                arrived(slab * WIDE + 2 * y + (1 - place % 2))

        limit = jnp.where(item == 2, SLABS - 1, jnp.where(item == 3, SLABS - 2, z))
        count = jnp.where(
            item >= 2, jnp.where(helper, 1, 0), jnp.where(jnp.logical_and(item == 1, giver), 1, 2)
        )
        base = jnp.where(item >= 2, 2 * item + 4, 4 * item)
        whole = jnp.logical_and(slab < limit, s >= 1)
        edge = slab == limit
        first = slab * WIDE

        for n in (2, 1):

            @pl.when(jnp.logical_and(count == n, whole))
            def _():
                body(first, WIDE, base, 2 * n, None)

            @pl.when(jnp.logical_and(count == n, jnp.logical_and(edge, s != 1)))
            def _():
                body(first + 2 * (place // 2), 2, base, 2 * n, (place % 2) * rows)

            low = jnp.logical_and(edge, jnp.logical_and(s != 0, place >= 2))

            @pl.when(jnp.logical_and(count == n, low))
            def _():
                body(first, 2, base, 2 * n, None)

        done = s == jnp.where(item == 2, lasts[1], jnp.where(item == 3, lasts[2], lasts[0]))
        for at, its, need in ((0, 0, 1), (1, 0, 2), (2, 1, 1), (3, 1, 2), (4, 2, 1), (5, 3, 1)):

            @pl.when(jnp.logical_and(done, jnp.logical_and(item == its, count >= need)))
            def _():
                finish(at)

        return carry

    lax.fori_loop(0, 4 * (SLABS + 1), step, 0)

    for p in range(pairs):

        @pl.when(kept > p)
        def _():
            own_piece(p).wait()
            for hop in range(1, heads_n):
                piece(p, p, hop, rank).wait_send()

        @pl.when(kept <= p)
        def _():
            piece(p, p, 0, rank).wait_recv()

        for hop in range(1, heads_n):
            piece(p, p, hop, rank).wait_recv()
    for n in range(2):

        @pl.when(helper)
        def _():
            for hop in range(heads_n):
                piece(pairs + n, pairs - 1, hop, sources[n]).wait_send()

        @pl.when(z == SLABS - 1 - n)
        def _():
            far_copy(n).wait_send()

    for n in range(2 * SLABS):
        send(mine, rank, mate, core_sem.at[n]).wait_send()
    for n in range(LINE):
        send(mine, rank, up, up_sem.at[n]).wait_send()
        send(mine, rank, down, down_sem.at[n]).wait_send()
        send(mine, rank, other, side_sem.at[n]).wait_send()


def local(heads_n, queries, keys, values, positions):
    rows = queries.shape[0]
    group = queries.shape[1] // HD
    cosine, sine_table = rotary_tables(positions, HD)
    cosines = jnp.concatenate([cosine, cosine], axis=1)
    sines = jnp.concatenate([-sine_table, sine_table], axis=1)
    tiles = group + group // 2
    ranks = SLABS * WIDE
    vmem = pl.BlockSpec(memory_space=pltpu.VMEM)
    dma = pltpu.SemaphoreType.DMA
    return pl.pallas_call(
        functools.partial(attend_kernel, heads_n),
        out_shape=jax.ShapeDtypeStruct((rows // heads_n, heads_n * group * HD), jnp.bfloat16),
        in_specs=[vmem] * 5,
        out_specs=vmem,
        scratch_shapes=[
            pltpu.VMEM((ranks, 2, rows, HD), jnp.bfloat16),
            pltpu.VMEM((rows, 2 * HD), jnp.bfloat16),
            pltpu.VMEM((2, rows, 2 * HD), jnp.bfloat16),
            pltpu.VMEM((tiles, rows, 2 * HD), jnp.bfloat16),
            pltpu.VMEM((tiles, rows, HD), jnp.float32),
            pltpu.VMEM((tiles, rows, HD), jnp.float32),
            pltpu.VMEM((tiles, rows, HD), jnp.float32),
            pltpu.VMEM((tiles // 2, rows, 2 * HD), jnp.bfloat16),
            dma((group // 2,)),
            dma((ranks,)),
            dma((LINE,)),
            dma((LINE,)),
            dma((LINE,)),
            dma((2 * SLABS,)),
            dma((2,)),
            dma((2,)),
            dma((tiles // 2, heads_n)),
            dma((group // 2, heads_n)),
        ],
        compiler_params=pltpu.CompilerParams(
            collective_id=0, has_side_effects=True, vmem_limit_bytes=60000 * 1024
        ),
    )(queries, keys, values, cosines, sines)


def solution(mesh):
    return jax.shard_map(
        functools.partial(local, mesh.shape["heads"]),
        mesh=mesh,
        in_specs=(P("ctx", "heads"), P("ctx", "heads"), P("ctx", "heads"), P("ctx")),
        out_specs=P(("ctx", "heads"), None),
        check_vma=False,
    )
```

time: 107 us -> 84.1 us (0.79)
  the two profiles are of different devices: /device:TPU:65 before, /device:TPU:241 now
where the time goes in v2:
time: 84.1 us; the launch traced here: 83.9 us
  Pallas kernels  79.4 us (94%)
  other arithmetic  2.4 us (3%)
  local copies, waits for them, and re-layouts  2.06 us (2%)
    pallas_call x1, Pallas kernels, local(): pl.pallas_call(functools.partial(attend_kernel, heads_n), out_shape=jax.S...  79.4 us
    unnamed x1, local copies, waits for them, and re-layouts  2.06 us

profile of v2, /device:TPU:241, one launch (start us, length us, event | category | flops | bytes accessed | tf_op | source)
XLA Modules:
  0.0 83.9 jit_solution(1448971075540935747)
XLA Ops:
  0.0 0.7 convert_element_type.3
  0.7 0.8 fusion
  1.5 0.9 %pad_maximum_fusion = (f32[384,128]{1,0:T(8,128)}, f32[384,128]{1,0:T(8,128)}) fusion(f32[384,64]{1,0:T(8,128)S(1)} %get-tuple-element.7, f32[384,64]{1,0:T(8,128)S(1)} %get-tuple-element.6, f32[384,64]{1,0:T(8,128)S(1)} %get-tuple-element.5), kind=kLoop, calls=%fused_computation.2 | loop fusion | flops 98304 | bytes 688128 | tf_op jit(solution)/shard_map/concatenate | solution.py:383
  2.4 79.4 %shard_map.46 = bf16[48,8192]{1,0:T(8,128)(2,1)} custom-call(bf16[384,1024]{1,0:T(8,128)(2,1)} %q_ref.1, bf16[384,128]{1,0:T(8,128)(2,1)} %k_ref.1, bf16[384,128]{1,0:T(8,128)(2,1)} %v_ref.1, f32[384,128]{1,0:T(8,128)} %get-tuple-element.8.cos_ref, f32[384,128]{1,0:T(8,128)} %get-tuple-element.9.sin_ref), custom_call_target="tpu_custom_call" | custom-call | tf_op jit(solution)/shard_map/pallas_call | solution.py:389
  81.8 2.1 %copy.6 = bf16[48,8192]{1,0:T(8,128)(2,1)} copy(bf16[48,8192]{1,0:T(8,128)(2,1)} %shard_map.46) | data formatting | bytes 1572864
  (1 shorter events, 0.0 us)
